TPU v7x, 512 devices: a whole 4x8x8 slice. The times are simulated.
512 devices in a mesh: row: 16 (over y, z_lo), col: 32 (over z_hi, x, core).
Axes of the slice: x: 4, y: 8, z: 8 (z_hi: 4, z_lo: 2; z = z_hi * 2 + z_lo), core: 2. Of those that a mesh axis runs over, the one named last changes fastest.
Arguments:
- tiles: bfloat16 [16, 32, 32, 256, 256], P('row', 'col'), may hold values from -6 to 6
- tile_ids: int32 [16, 32, 2, 32], P('row', 'col'), may hold values from 0 to 7, as said below
- tile_count: int32 [16, 32], P('row', 'col'), may hold values from 8 to 32
- query_degree: int32 [32768], P('row'), may hold values from 1 to 32
- product_degree: int32 [65536], P('col'), may hold values from 1 to 32
- panel: float32 [64, 65536], P(None, ('col', 'row')), may hold values from -6 to 6
Outputs:
- basis: float32 [64, 65536], P(None, ('col', 'row'))
Inputs may be any that keep to these rules, and one draw needn't show every extreme that they name: `tile_ids`: on each device the 32 (tile row, tile column) pairs are distinct; tile row is below 8 and tile column below 8.
All inputs are finite; a program needn't handle non-finite values.
Results may differ from a plain program's by a relative error of at most 0.0042.
Values may be sent and summed in bfloat16 or wider, within the bound.
A program may use at most 64 MiB of HBM per device.

v0:
```python
import math
import jax
import jax.numpy as jnp
from jax import lax
from jax.sharding import PartitionSpec as P

ITERS = 2
HIGH = lax.Precision.HIGHEST


def orthonormal(lifted, gram):
    lower = jnp.linalg.cholesky(gram)
    return lax.linalg.triangular_solve(lower, lifted, left_side=True, lower=True)


def shards(tiles, tile_ids, tile_count, query_degree, product_degree, panel):
    tile_set = tiles[0, 0]
    slot_ids = tile_ids[0, 0]
    live_count = tile_count[0, 0]
    slots = tile_set.shape[0]
    side = tile_set.shape[1]
    width = panel.shape[0]
    query_tiles = query_degree.shape[0] // side
    product_tiles = product_degree.shape[0] // side
    live_slot = (jnp.arange(slots, dtype=jnp.int32) < live_count).astype(jnp.float32)
    row_hot = (slot_ids[0][:, None] == jnp.arange(query_tiles, dtype=jnp.int32)[None, :]).astype(
        jnp.float32
    ) * live_slot[:, None]
    col_hot = (slot_ids[1][:, None] == jnp.arange(product_tiles, dtype=jnp.int32)[None, :]).astype(
        jnp.float32
    ) * live_slot[:, None]
    qscale = 1.0 / jnp.sqrt(query_degree.astype(jnp.float32))
    pscale = 1.0 / jnp.sqrt(product_degree.astype(jnp.float32))
    row_at = lax.axis_index("row")
    col_at = lax.axis_index("col")
    share = panel.shape[1]
    my_pscale = lax.dynamic_slice_in_dim(pscale, row_at * share, share)
    root_count = math.sqrt(product_degree.shape[0] * lax.axis_size("col"))
    current = panel
    for iteration in range(ITERS):
        scaled = (current * my_pscale[None, :]).astype(jnp.bfloat16)
        scaled_block = lax.all_gather(scaled, "row", axis=1, tiled=True)
        picked = jnp.take(scaled_block.reshape(width, product_tiles, side), slot_ids[1], axis=1)
        products = jnp.einsum("rkj,kij->kri", picked, tile_set, preferred_element_type=jnp.float32)
        partial_sum = jnp.einsum("kq,kri->rqi", row_hot, products, precision=HIGH).reshape(
            width, query_tiles * side
        )
        query_share = lax.psum_scatter(partial_sum, "col", scatter_dimension=1, tiled=True)
        columns = query_share.shape[1]
        my_qscale = lax.dynamic_slice_in_dim(qscale, col_at * columns, columns)
        rounded = (query_share * my_qscale[None, :]).astype(jnp.bfloat16)
        query_block = lax.all_gather(rounded, "col", axis=1, tiled=True)
        backward_picked = jnp.take(
            query_block.reshape(width, query_tiles, side), slot_ids[0], axis=1
        )
        backward_products = jnp.einsum(
            "rki,kij->krj", backward_picked, tile_set, preferred_element_type=jnp.float32
        )
        lifted = (
            lax.psum_scatter(
                jnp.einsum("kp,krj->rpj", col_hot, backward_products, precision=HIGH).reshape(
                    width, product_tiles * side
                ),
                "row",
                scatter_dimension=1,
                tiled=True,
            )
            * my_pscale[None, :]
        )
        gram = lax.psum(jnp.einsum("ri,si->rs", lifted, lifted, precision=HIGH), ("row", "col"))
        current = orthonormal(lifted, gram)
    return current * root_count


def solution(mesh):
    in_specs = (
        P("row", "col", None, None, None),
        P("row", "col", None, None),
        P("row", "col"),
        P("row"),
        P("col"),
        P(None, ("col", "row")),
    )
    out_specs = P(None, ("col", "row"))
    return jax.shard_map(shards, mesh=mesh, in_specs=in_specs, out_specs=out_specs, check_vma=False)
```

profile of v0, /device:TPU:24, one launch (start us, length us, event | category | flops | bytes accessed | tf_op | source)
XLA Modules:
  0.0 757.7 jit_solution(1532699937566994767)
XLA Ops:
  6.5 0.8 slice_bitcast_fusion.1
  7.3 0.8 compare_and_fusion
  8.7 0.8 fusion.78
  9.5 0.8 multiply_convert_fusion.2
  10.3 32.3 %all_gather.12 = bf16[64,2048]{1,0:T(8,128)(2,1)S(1)} all-gather(bf16[64,128]{1,0:T(8,128)(2,1)S(1)} %multiply_convert_fusion.2), channel_id=1, replica_groups=mesh['row'=16,'col'=32] {'row'}, dimensions={1}, use_global_device_ids=true | all-gather | bytes 278528 | tf_op jit(solution)/shard_map/all_gather | solution.py:42
  42.6 0.6 gather_fusion
  43.2 3.6 fusion.6
  46.8 2.4 fusion.16
  49.1 1.4 copy.55
  50.6 0.8 fusion.77
  51.3 101.7 %reduce-scatter.13.cloned.1.call-done = f32[64,64]{1,0:T(8,128)} async-done(((f32[2048,64]{1,0:T(8,128)}), f32[64,64]{1,0:T(8,128)}) %reduce-scatter.13.cloned.1.call-update) | async-done | bytes 16400
  153.1 0.8 copy.52
  153.9 0.1 copy.31
  154.0 43.8 %all_gather.13 = bf16[64,2048]{0,1:T(8,128)(2,1)S(1)} all-gather(bf16[64,64]{0,1:T(8,128)(2,1)S(1)} %copy.31), channel_id=1, replica_groups=mesh['row'=16,'col'=32] {'col'}, dimensions={1}, use_global_device_ids=true | all-gather | bytes 270336 | tf_op jit(solution)/shard_map/all_gather | solution.py:52
  197.8 0.2 copy.33
  198.0 0.6 gather_fusion.1
  198.6 3.1 fusion.4
  201.7 2.4 fusion.12
  204.1 1.0 copy.59
  205.1 67.3 %reduce-scatter.9.cloned.1.call-done = f32[64,128]{1,0:T(8,128)} async-done(((f32[64,2048]{1,0:T(8,128)}), f32[64,128]{1,0:T(8,128)}) %reduce-scatter.9.cloned.1.call-update) | async-done | bytes 32784 | tf_op jit(solution)/shard_map/reduce_scatter | solution.py:60
  272.4 1.0 fusion.51
  273.4 98.9 %psum.14 = f32[64,64]{0,1:T(8,128)S(1)} all-reduce(f32[64,64]{0,1:T(8,128)S(1)} %fusion.51), channel_id=1, replica_groups=mesh['row'=16,'col'=32] {'row','col'}, use_global_device_ids=true, to_apply=%region_2.4 | all-reduce | flops 4096 | bytes 32768 | tf_op jit(solution)/shard_map/psum | solution.py:70
  372.5 5.8 cholesky.44
  378.3 0.6 compare_reduce_fusion.1
  379.0 0.7 fusion.39
  379.6 4.9 custom-call.6
  384.5 1.0 fusion.22
  385.6 29.2 %all_gather.14 = bf16[64,2048]{1,0:T(8,128)(2,1)S(1)} all-gather(bf16[64,128]{1,0:T(8,128)(2,1)S(1)} %fusion.22), channel_id=1, replica_groups=mesh['row'=16,'col'=32] {'row'}, dimensions={1}, use_global_device_ids=true | all-gather | bytes 278528 | tf_op jit(solution)/shard_map/all_gather | solution.py:42
  414.8 0.6 gather_fusion.2
  415.4 3.6 fusion.2
  419.0 2.4 fusion.19
  421.4 1.4 copy.56
  422.8 95.3 %reduce-scatter.15.cloned.1.call-done = f32[64,64]{1,0:T(8,128)} async-done(((f32[2048,64]{1,0:T(8,128)}), f32[64,64]{1,0:T(8,128)}) %reduce-scatter.15.cloned.1.call-update) | async-done | bytes 16400
  518.1 0.8 copy.54
  519.0 43.8 %all_gather.15 = bf16[64,2048]{0,1:T(8,128)(2,1)S(1)} all-gather(bf16[64,64]{0,1:T(8,128)(2,1)S(1)} %copy.39), channel_id=1, replica_groups=mesh['row'=16,'col'=32] {'col'}, dimensions={1}, use_global_device_ids=true | all-gather | bytes 270336 | tf_op jit(solution)/shard_map/all_gather | solution.py:52
  562.8 0.2 copy.41
  563.0 0.6 gather_fusion.3
  563.6 3.1 fusion
  566.7 2.4 fusion.8
  569.1 1.0 copy.60
  570.1 67.3 %reduce-scatter.11.cloned.1.call-done = f32[64,128]{1,0:T(8,128)} async-done(((f32[64,2048]{1,0:T(8,128)}), f32[64,128]{1,0:T(8,128)}) %reduce-scatter.11.cloned.1.call-update) | async-done | bytes 32784 | tf_op jit(solution)/shard_map/reduce_scatter | solution.py:60
  637.4 1.0 fusion.48
  638.4 99.0 %psum.15 = f32[64,64]{0,1:T(8,128)S(1)} all-reduce(f32[64,64]{0,1:T(8,128)S(1)} %fusion.48), channel_id=1, replica_groups=mesh['row'=16,'col'=32] {'row','col'}, use_global_device_ids=true, to_apply=%region_7.11 | all-reduce | flops 4096 | bytes 32768 | tf_op jit(solution)/shard_map/psum | solution.py:70
  737.5 5.8 cholesky.55
  743.4 0.6 compare_reduce_fusion
  744.0 0.7 fusion.40
  744.7 4.9 custom-call.7
  749.6 1.6 convolution_multiply_fusion
  (22 shorter events, 0.6 us)
Async XLA Ops:
  6.5 146.5 %reduce-scatter.13.cloned.1.call-start = ((), (), s32[]{:S(2)}) async-start(), calls=%async_computation.6 | async-start | bytes 1081344
  50.5 221.9 %reduce-scatter.9.cloned.1.call-start = ((), (), s32[]{:S(2)}) async-start(), calls=%async_computation.4 | async-start | bytes 557056 | tf_op jit(solution)/shard_map/reduce_scatter | solution.py:60
  205.0 313.1 %reduce-scatter.15.cloned.1.call-start = ((), (), s32[]{:S(2)}) async-start(), calls=%async_computation.7 | async-start | bytes 1081344
  422.8 214.6 %reduce-scatter.11.cloned.1.call-start = ((), (), s32[]{:S(2)}) async-start(), calls=%async_computation.5 | async-start | bytes 557056 | tf_op jit(solution)/shard_map/reduce_scatter | solution.py:60
Sparse Core Ops, SparseCore 0:
  50.6 102.3 reduce-scatter.12
  205.2 67.2 reduce-scatter.8
  422.9 95.1 reduce-scatter.14
  570.2 67.1 reduce-scatter.10
where the time goes:
time: 759 us; the launch traced here: 758 us
  blocking collectives  347 us (46%)
  waiting for transfers between devices  332 us (44%)
  matrix products  27.4 us (4%)
  other arithmetic  27.3 us (4%)
  between operations  14 us (2%)
  local copies, waits for them, and re-layouts  10.3 us (1%)
    psum x2, blocking collectives, shards(): lax.psum(jnp.einsum('ri,si->rs', lifted, lifted, precision=HIGH), ('row',...  198 us
    unnamed x6, waiting for transfers between devices  197 us
    reduce_scatter x2, waiting for transfers between devices, shards(): lax.psum_scatter(jnp.einsum('kp,krj->rpj', col_hot, backward_products, pr...  135 us
    all_gather x2, blocking collectives, shards(): query_block = lax.all_gather(rounded, 'col', axis=1, tiled=True)  87.6 us
    all_gather x2, blocking collectives, shards(): scaled_block = lax.all_gather(scaled, 'row', axis=1, tiled=True)  61.5 us
  transfers between devices with their start and end apart: 4, of which 4 were waited for; matrix products, arithmetic and copies ran while one was open for 0% of the time, Pallas kernels for 0%

commit v1 on v0

--- a/solution.py
+++ b/solution.py
@@ -67,7 +67,9 @@
             )
             * my_pscale[None, :]
         )
-        gram = lax.psum(jnp.einsum("ri,si->rs", lifted, lifted, precision=HIGH), ("row", "col"))
+        gram = lax.psum(
+            lax.psum(jnp.einsum("ri,si->rs", lifted, lifted, precision=HIGH), "col"), "row"
+        )
         current = orthonormal(lifted, gram)
     return current * root_count
 

time: 759 us -> 966 us (1.27)
  the two profiles are of different devices: /device:TPU:24 before, /device:TPU:32 now
where the time goes in v1:
time: 966 us; the launch traced here: 965 us
  blocking collectives  554 us (57%)
  waiting for transfers between devices  332 us (34%)
  matrix products  27.4 us (3%)
  other arithmetic  27.3 us (3%)
  between operations  14 us (1%)
  local copies, waits for them, and re-layouts  10.3 us (1%)
    psum x2, blocking collectives, shards(): lax.psum(jnp.einsum('ri,si->rs', lifted, lifted, precision=HIGH), 'col')  276 us
    unnamed x6, waiting for transfers between devices  197 us
    reduce_scatter x2, waiting for transfers between devices, shards(): lax.psum_scatter(jnp.einsum('kp,krj->rpj', col_hot, backward_products, pr...  135 us
    psum x2, blocking collectives, shards(): lax.psum(lax.psum(jnp.einsum('ri,si->rs', lifted, lifted, precision=HIGH)...  126 us
    all_gather x2, blocking collectives, shards(): query_block = lax.all_gather(rounded, 'col', axis=1, tiled=True)  87.6 us
    all_gather x2, blocking collectives, shards(): scaled_block = lax.all_gather(scaled, 'row', axis=1, tiled=True)  64.5 us
  transfers between devices with their start and end apart: 4, of which 4 were waited for; matrix products, arithmetic and copies ran while one was open for 0% of the time, Pallas kernels for 0%

profile of v1, /device:TPU:32, one launch (start us, length us, event | category | flops | bytes accessed | tf_op | source)
XLA Modules:
  0.0 965.3 jit_solution(204942643055748337)
XLA Ops:
  6.5 0.8 slice_bitcast_fusion.1
  7.3 0.8 compare_and_fusion
  8.7 0.8 fusion.78
  9.5 0.8 multiply_convert_fusion.2
  10.3 33.4 %all_gather.12 = bf16[64,2048]{1,0:T(8,128)(2,1)S(1)} all-gather(bf16[64,128]{1,0:T(8,128)(2,1)S(1)} %multiply_convert_fusion.2), channel_id=1, replica_groups=mesh['row'=16,'col'=32] {'row'}, dimensions={1}, use_global_device_ids=true | all-gather | bytes 278528 | tf_op jit(solution)/shard_map/all_gather | solution.py:42
  43.7 0.6 gather_fusion
  44.3 3.6 fusion.6
  47.9 2.4 fusion.16
  50.2 1.4 copy.55
  51.7 0.8 fusion.77
  52.4 100.5 %reduce-scatter.13.cloned.1.call-done = f32[64,64]{1,0:T(8,128)} async-done(((f32[2048,64]{1,0:T(8,128)}), f32[64,64]{1,0:T(8,128)}) %reduce-scatter.13.cloned.1.call-update) | async-done | bytes 16400
  153.0 0.8 copy.52
  153.9 43.8 %all_gather.13 = bf16[64,2048]{0,1:T(8,128)(2,1)S(1)} all-gather(bf16[64,64]{0,1:T(8,128)(2,1)S(1)} %copy.31), channel_id=1, replica_groups=mesh['row'=16,'col'=32] {'col'}, dimensions={1}, use_global_device_ids=true | all-gather | bytes 270336 | tf_op jit(solution)/shard_map/all_gather | solution.py:52
  197.7 0.2 copy.33
  197.9 0.6 gather_fusion.1
  198.5 3.1 fusion.4
  201.6 2.4 fusion.12
  203.9 1.0 copy.59
  205.0 67.3 %reduce-scatter.9.cloned.1.call-done = f32[64,128]{1,0:T(8,128)} async-done(((f32[64,2048]{1,0:T(8,128)}), f32[64,128]{1,0:T(8,128)}) %reduce-scatter.9.cloned.1.call-update) | async-done | bytes 32784 | tf_op jit(solution)/shard_map/reduce_scatter | solution.py:60
  272.3 1.0 fusion.51
  273.3 138.2 %psum.28 = f32[64,64]{0,1:T(8,128)S(1)} all-reduce(f32[64,64]{0,1:T(8,128)S(1)} %fusion.51), channel_id=1, replica_groups=mesh['row'=16,'col'=32] {'col'}, use_global_device_ids=true, to_apply=%region_2.4 | all-reduce | flops 4096 | bytes 32768 | tf_op jit(solution)/shard_map/psum | solution.py:71
  411.5 63.0 %psum.29 = f32[64,64]{0,1:T(8,128)S(1)} all-reduce(f32[64,64]{0,1:T(8,128)S(1)} %psum.28), channel_id=1, replica_groups=mesh['row'=16,'col'=32] {'row'}, use_global_device_ids=true, to_apply=%region_3.5 | all-reduce | flops 4096 | bytes 32768 | tf_op jit(solution)/shard_map/psum | solution.py:70
  474.6 5.8 cholesky.44
  480.5 0.6 compare_reduce_fusion.1
  481.1 0.7 fusion.39
  481.8 4.9 custom-call.6
  486.7 1.0 fusion.22
  487.7 31.1 %all_gather.14 = bf16[64,2048]{1,0:T(8,128)(2,1)S(1)} all-gather(bf16[64,128]{1,0:T(8,128)(2,1)S(1)} %fusion.22), channel_id=1, replica_groups=mesh['row'=16,'col'=32] {'row'}, dimensions={1}, use_global_device_ids=true | all-gather | bytes 278528 | tf_op jit(solution)/shard_map/all_gather | solution.py:42
  518.8 0.6 gather_fusion.2
  519.4 3.6 fusion.2
  523.0 2.4 fusion.19
  525.4 1.4 copy.56
  526.8 96.5 %reduce-scatter.15.cloned.1.call-done = f32[64,64]{1,0:T(8,128)} async-done(((f32[2048,64]{1,0:T(8,128)}), f32[64,64]{1,0:T(8,128)}) %reduce-scatter.15.cloned.1.call-update) | async-done | bytes 16400
  623.3 0.8 copy.54
  624.3 43.8 %all_gather.15 = bf16[64,2048]{0,1:T(8,128)(2,1)S(1)} all-gather(bf16[64,64]{0,1:T(8,128)(2,1)S(1)} %copy.39), channel_id=1, replica_groups=mesh['row'=16,'col'=32] {'col'}, dimensions={1}, use_global_device_ids=true | all-gather | bytes 270336 | tf_op jit(solution)/shard_map/all_gather | solution.py:52
  668.3 0.6 gather_fusion.3
  668.9 3.1 fusion
  672.0 2.4 fusion.8
  674.3 1.0 copy.60
  675.3 67.4 %reduce-scatter.11.cloned.1.call-done = f32[64,128]{1,0:T(8,128)} async-done(((f32[64,2048]{1,0:T(8,128)}), f32[64,128]{1,0:T(8,128)}) %reduce-scatter.11.cloned.1.call-update) | async-done | bytes 32784 | tf_op jit(solution)/shard_map/reduce_scatter | solution.py:60
  742.7 1.0 fusion.48
  743.8 138.2 %psum.30 = f32[64,64]{0,1:T(8,128)S(1)} all-reduce(f32[64,64]{0,1:T(8,128)S(1)} %fusion.48), channel_id=1, replica_groups=mesh['row'=16,'col'=32] {'col'}, use_global_device_ids=true, to_apply=%region_8.0 | all-reduce | flops 4096 | bytes 32768 | tf_op jit(solution)/shard_map/psum | solution.py:71
  881.9 63.0 %psum.31 = f32[64,64]{0,1:T(8,128)S(1)} all-reduce(f32[64,64]{0,1:T(8,128)S(1)} %psum.30), channel_id=1, replica_groups=mesh['row'=16,'col'=32] {'row'}, use_global_device_ids=true, to_apply=%region_9.13 | all-reduce | flops 4096 | bytes 32768 | tf_op jit(solution)/shard_map/psum | solution.py:70
  945.1 5.8 cholesky.55
  950.9 0.6 compare_reduce_fusion
  951.6 0.7 fusion.40
  952.2 4.9 custom-call.7
  957.1 1.6 convolution_multiply_fusion
  (24 shorter events, 0.9 us)
Async XLA Ops:
  6.5 146.4 %reduce-scatter.13.cloned.1.call-start = ((), (), s32[]{:S(2)}) async-start(), calls=%async_computation.6 | async-start | bytes 1081344
  51.6 220.7 %reduce-scatter.9.cloned.1.call-start = ((), (), s32[]{:S(2)}) async-start(), calls=%async_computation.4 | async-start | bytes 557056 | tf_op jit(solution)/shard_map/reduce_scatter | solution.py:60
  204.9 418.4 %reduce-scatter.15.cloned.1.call-start = ((), (), s32[]{:S(2)}) async-start(), calls=%async_computation.7 | async-start | bytes 1081344
  526.8 216.0 %reduce-scatter.11.cloned.1.call-start = ((), (), s32[]{:S(2)}) async-start(), calls=%async_computation.5 | async-start | bytes 557056 | tf_op jit(solution)/shard_map/reduce_scatter | solution.py:60
Sparse Core Ops, SparseCore 0:
  51.7 101.1 reduce-scatter.12
  205.0 67.1 reduce-scatter.8
  526.9 96.3 reduce-scatter.14
  675.4 67.2 reduce-scatter.10
